TPU v7x, 256 devices: a whole 4x4x8 slice. The times are simulated.
256 devices in a mesh: tmpl: 32 (over x, z_lo, core), tm: 8 (over y, z_hi).
Axes of the slice: x: 4, y: 4, z: 8 (z_hi: 2, z_lo: 4; z = z_hi * 4 + z_lo), core: 2. Of those that a mesh axis runs over, the one named last changes fastest.
Arguments:
- records: bfloat16 [1536, 4096], P('tmpl', 'tm'), may hold values from -6 to 6
- templates: bfloat16 [2, 1024, 48, 200], P(None, 'tmpl'), may hold values from -0.0625 to 0.0625
- channels: int32 [2, 1024, 48], P(None, 'tmpl'), may hold values from 0 to 1535
- moveouts: int32 [2, 1024, 48], P(None, 'tmpl'), may hold values from 0 to 55
Outputs:
- detections: float32 [2, 1024, 4096], P(None, 'tmpl', 'tm')
All inputs are finite; a program needn't handle non-finite values.
Results may differ from a plain program's by a relative error of at most 0.0043.
Values may be sent and summed in bfloat16 or wider, within the bound.
No kernel may reach another device: no remote copies, remote signals or barrier semaphores. Data moves between devices by JAX's collectives and lax.ppermute only.
A program may use at most 64 MiB of HBM per device.

v0:
```python
import math
import jax
import jax.numpy as jnp
from jax import lax
from jax.sharding import PartitionSpec as P

L = 200
LAGS = 56


def from_behind(block, axis, distance):
    devices = range(lax.axis_size(axis))
    route = [(i - distance, i) for i in devices if i - distance in devices]
    return lax.ppermute(block, axis, route)


def tables(count, freqs, width):
    sample = jnp.arange(count, dtype=jnp.int32)[:, None]
    freq = jnp.arange(freqs, dtype=jnp.int32)[None, :]
    angle = 2.0 * math.pi / width * (sample * freq % width).astype(jnp.float32)
    return jnp.concatenate([jnp.cos(angle), jnp.sin(angle)], axis=1)


def detect(waves, chans, lags, spectra, forward, inverse, weight, freq, width, freqs):
    count = waves.shape[0]
    hspec = jnp.dot(
        waves.reshape(-1, waves.shape[2]),
        forward[: waves.shape[2]],
        preferred_element_type=jnp.float32,
    )
    h_cos, h_sin = (hspec[:, :freqs], hspec[:, freqs:])
    angle = (
        2.0
        * math.pi
        / width
        * (lags.reshape(-1)[:, None] * freq[None, :] % width).astype(jnp.float32)
    )
    c_theta, s_theta = (jnp.cos(angle), jnp.sin(angle))
    picked = spectra[chans.reshape(-1)].astype(jnp.float32)
    x_cos, x_sin = (picked[:, :freqs], picked[:, freqs:])
    prod_a = h_cos * x_cos + h_sin * x_sin
    prod_b = h_sin * x_cos - h_cos * x_sin
    real_part = (prod_a * c_theta - prod_b * s_theta).reshape(count, -1, freqs).sum(axis=1)
    imag_part = (prod_a * s_theta + prod_b * c_theta).reshape(count, -1, freqs).sum(axis=1)
    joint = jnp.concatenate([real_part * weight, -imag_part * weight], axis=1)
    return lax.dot_general(
        joint, inverse, (((1,), (1,)), ((), ())), precision=lax.Precision.HIGHEST
    )


def per_device(records, templates, channels, moveouts):
    time_dev = records.shape[1]
    extra = L + LAGS - 2
    width = time_dev + extra
    freqs = width // 2 + 1
    forward = tables(width, freqs, width).astype(jnp.bfloat16)
    inverse = tables(time_dev, freqs, width)
    freq = jnp.arange(freqs, dtype=jnp.int32)
    weight = jnp.where((freq == 0) | (freq == freqs - 1), 1.0, 2.0).astype(jnp.float32) / width
    rim = from_behind(records[:, :extra], "tm", -1)
    window = jnp.concatenate([records, rim], axis=1)
    spectra = jnp.dot(
        lax.all_gather(window, "tmpl", axis=0, tiled=True),
        forward,
        preferred_element_type=jnp.float32,
    ).astype(jnp.bfloat16)
    results = []
    for batch in range(templates.shape[0]):
        results.append(
            detect(
                templates[batch],
                channels[batch],
                moveouts[batch],
                spectra,
                forward,
                inverse,
                weight,
                freq,
                width,
                freqs,
            )
        )
    return jnp.stack(results)


def solution(mesh):
    placed = (
        P("tmpl", "tm"),
        P(None, "tmpl", None, None),
        P(None, "tmpl", None),
        P(None, "tmpl", None),
    )
    return jax.shard_map(
        per_device, mesh=mesh, in_specs=placed, out_specs=P(None, "tmpl", "tm"), check_vma=False
    )
```

profile of v0, /device:TPU:1, one launch (start us, length us, event | category | flops | bytes accessed | tf_op | source)
XLA Modules:
  0.0 185.4 jit_solution(2177436032640914762)
XLA Ops:
  8.7 9.6 %collective-permute-done = bf16[48,254]{1,0:T(8,128)(2,1)S(1)} collective-permute-done((bf16[48,254]{1,0:T(8,128)(2,1)S(1)}, bf16[48,254]{1,0:T(8,128)(2,1)S(1)}, u32[]{:S(2)}, u32[]{:S(2)}) %collective-permute-start) | collective-permute-done | bytes 24416 | tf_op jit(solution)/shard_map/ppermute | solution.py:14
  21.6 5.0 %sine_convert_fusion = (bf16[766,384]{1,0:T(8,128)(2,1)S(1)}, bf16[766,384]{1,0:T(8,128)(2,1)S(1)}) fusion(), kind=kLoop, calls=%fused_computation.41 | loop fusion | flops 3235584 | bytes 1176576 | tf_op jit(solution)/shard_map/convert.1
  27.7 4.2 %fusion.30 = (f32[512,384]{1,0:T(8,128)S(1)}, f32[512,384]{1,0:T(8,128)}) fusion(), kind=kLoop, calls=%fused_computation.54 | loop fusion | flops 1769472 | bytes 1572864 | tf_op jit(solution)/shard_map/sin | solution.py:21
  32.1 3.0 %convolution_bitcast_fusion = f32[1536,768]{0,1:T(8,128)} fusion(bf16[200,768]{1,0:T(8,128)(2,1)S(1)} %pad_maximum_fusion.7, bf16[1536,200]{1,0:T(8,128)(2,1)S(1)} %bitcast.24), kind=kOutput, calls=%fused_computation.2 | convolution fusion | flops 471859200 | bytes 5640192 | tf_op jit(solution)/shard_map/dot_general | solution.py:26
  35.1 3.0 %convolution_bitcast_fusion.1 = f32[1536,768]{0,1:T(8,128)} fusion(bf16[200,768]{1,0:T(8,128)(2,1)S(1)} %pad_maximum_fusion.7, bf16[1536,200]{1,0:T(8,128)(2,1)S(1)} %bitcast.23), kind=kOutput, calls=%fused_computation.3 | convolution fusion | flops 471859200 | bytes 5640192 | tf_op jit(solution)/shard_map/dot_general | solution.py:26
  38.0 46.4 %all-gather.2.cloned.1.call-done = bf16[1536,766]{1,0:T(8,128)(2,1)} async-done(((bf16[48,766]{1,0:T(8,128)(2,1)}), bf16[1536,766]{1,0:T(8,128)(2,1)}) %all-gather.2.cloned.1.call-update) | async-done | bytes 2353168 | tf_op jit(solution)/shard_map/all_gather | solution.py:63
  84.4 4.0 %convolution_convert_fusion = bf16[1536,768]{1,0:T(8,128)(2,1)S(1)} fusion(bf16[1536,766]{1,0:T(8,128)(2,1)} %all-gather.2.cloned.1.call-done, bf16[766,384]{1,0:T(8,128)(2,1)} %copy-done.3, bf16[766,384]{1,0:T(8,128)(2,1)} %copy-done.4), kind=kOutput, calls=%fused_computation.6 | convolution fusion | flops 1810753536 | bytes 5889024 | tf_op jit(solution)/shard_map/dot_general | solution.py:62
  88.4 5.7 %gather_fusion.1 = bf16[1536,768]{1,0:T(8,128)(2,1)} fusion(bf16[1536,768]{1,0:T(8,128)(2,1)S(1)} %convolution_convert_fusion, s32[2048]{0:T(1024)S(1)} %pad_clamp_fusion), kind=kCustom, calls=%fused_computation.1 | custom fusion | bytes 4724736 | tf_op jit(solution)/shard_map/gather | solution.py:39
  94.1 4.3 %copy.10 = bf16[1536,768]{0,1:T(8,128)(2,1)} copy(bf16[1536,768]{1,0:T(8,128)(2,1)} %gather_fusion.1) | data formatting | bytes 4718592 | tf_op jit(solution)/shard_map/gather | solution.py:39
  98.3 2.3 %convert_element_type.31 = f32[1536,768]{0,1:T(8,128)S(1)} convert(bf16[1536,768]{0,1:T(8,128)(2,1)} %copy.10) | non-fusion elementwise | flops 1179648 | bytes 7077888 | tf_op jit(solution)/shard_map/convert_element_type | solution.py:39
  100.6 13.5 %multiply_subtract_fusion = (f32[1536,384]{0,1:T(8,128)}, f32[1536,384]{0,1:T(8,128)S(1)}, f32[1536,384]{0,1:T(8,128)S(1)}) fusion(s32[1536]{0:T(1024)S(1)} %mul.198, f32[1536,768]{0,1:T(8,128)S(1)} %convert_element_type.31, f32[1536,768]{0,1:T(8,128)} %convolution_bitcast_fusion), kind=kLoop, calls=%fused_computation.12 | loop fusion | flops 10616832 | bytes 16521216 | tf_op jit(solution)/shard_map/sub | solution.py:43
  114.1 10.8 %multiply_add_fusion = f32[1536,384]{0,1:T(8,128)} fusion(f32[1536,384]{0,1:T(8,128)S(1)} %get-tuple-element.10, f32[1536,384]{0,1:T(8,128)S(1)} %get-tuple-element.9, s32[1536]{0:T(1024)S(1)} %mul.198), kind=kLoop, calls=%fused_computation.11 | loop fusion | flops 7077888 | bytes 7084032 | tf_op jit(solution)/shard_map/add | solution.py:44
  124.9 3.1 %copy.12 = f32[1536,384]{1,0:T(8,128)} copy(f32[1536,384]{0,1:T(8,128)} %multiply_add_fusion) | data formatting | bytes 4718592 | tf_op jit(solution)/shard_map/add | solution.py:44
  128.1 5.7 %gather_fusion = bf16[1536,768]{1,0:T(8,128)(2,1)} fusion(bf16[1536,768]{1,0:T(8,128)(2,1)S(1)} %convolution_convert_fusion, s32[2048]{0:T(1024)S(1)} %pad_clamp_fusion.1), kind=kCustom, calls=%fused_computation | custom fusion | bytes 4724736 | tf_op jit(solution)/shard_map/gather | solution.py:39
  133.7 2.8 %copy.7 = bf16[1536,768]{0,1:T(8,128)(2,1)S(1)} copy(bf16[1536,768]{1,0:T(8,128)(2,1)} %gather_fusion) | data formatting | bytes 4718592 | tf_op jit(solution)/shard_map/gather | solution.py:39
  137.2 13.5 %multiply_subtract_fusion.2 = (f32[1536,384]{0,1:T(8,128)}, f32[1536,384]{0,1:T(8,128)S(1)}, f32[1536,384]{0,1:T(8,128)S(1)}) fusion(s32[1536]{0:T(1024)S(1)} %mul.177, f32[1536,768]{0,1:T(8,128)S(1)} %convert_element_type.28, f32[1536,768]{0,1:T(8,128)} %convolution_bitcast_fusion.1), kind=kLoop, calls=%fused_computation.21 | loop fusion | flops 10616832 | bytes 16521216 | tf_op jit(solution)/shard_map/sub | solution.py:43
  150.7 9.9 %multiply_add_fusion.2 = f32[1536,384]{0,1:T(8,128)S(1)} fusion(f32[1536,384]{0,1:T(8,128)S(1)} %get-tuple-element.7, f32[1536,384]{0,1:T(8,128)S(1)} %get-tuple-element.6, s32[1536]{0:T(1024)S(1)} %mul.177), kind=kLoop, calls=%fused_computation.20 | loop fusion | flops 7077888 | bytes 7084032 | tf_op jit(solution)/shard_map/add | solution.py:44
  160.6 2.0 %copy.9 = f32[1536,384]{1,0:T(8,128)} copy(f32[1536,384]{0,1:T(8,128)S(1)} %multiply_add_fusion.2) | data formatting | bytes 4718592 | tf_op jit(solution)/shard_map/add | solution.py:44
  162.6 2.0 %reduce_sum.39 = f32[32,384]{1,0:T(8,128)S(1)} reduce(f32[32,48,384]{2,1,0:T(8,128)} %bitcast.19, f32[]{:T(128)} %constant.26.clone.1), dimensions={1}, to_apply=%region_3.4 | reduce | flops 577536 | bytes 2408452 | tf_op jit(solution)/shard_map/reduce_sum | solution.py:44
  164.6 1.9 %reduce_sum.37 = f32[32,384]{1,0:T(8,128)S(1)} reduce(f32[32,48,384]{2,1,0:T(8,128)} %bitcast.20, f32[]{:T(128)} %constant.26.clone.1), dimensions={1}, to_apply=%region_1.2 | reduce | flops 577536 | bytes 2408452 | tf_op jit(solution)/shard_map/reduce_sum | solution.py:44
  166.5 2.0 %copy.11 = f32[1536,384]{1,0:T(8,128)} copy(f32[1536,384]{0,1:T(8,128)S(1)} %copy-done) | data formatting | bytes 4718592 | tf_op jit(solution)/shard_map/sub | solution.py:43
  168.5 2.0 %reduce_sum.38 = f32[32,384]{1,0:T(8,128)S(1)} reduce(f32[32,48,384]{2,1,0:T(8,128)} %bitcast.22, f32[]{:T(128)} %constant.26.clone.1), dimensions={1}, to_apply=%region_2.3 | reduce | flops 577536 | bytes 2408452 | tf_op jit(solution)/shard_map/reduce_sum | solution.py:43
  170.8 2.0 %copy.8 = f32[1536,384]{1,0:T(8,128)} copy(f32[1536,384]{0,1:T(8,128)S(1)} %copy-done.1) | data formatting | bytes 4718592 | tf_op jit(solution)/shard_map/sub | solution.py:43
  172.8 1.9 %reduce_sum.36 = f32[32,384]{1,0:T(8,128)S(1)} reduce(f32[32,48,384]{2,1,0:T(8,128)} %bitcast.21, f32[]{:T(128)} %constant.26.clone.1), dimensions={1}, to_apply=%region_0.1 | reduce | flops 577536 | bytes 2408452 | tf_op jit(solution)/shard_map/reduce_sum | solution.py:43
  (35 shorter events, 11.4 us)
Async XLA Ops:
  6.5 77.9 %all-gather.2.cloned.1.call-start = ((), (), s32[]{:S(2)}) async-start(), calls=%async_computation | async-start | bytes 2433024 | tf_op jit(solution)/shard_map/all_gather | solution.py:63
  7.3 24.7 %copy-start.5 = (bf16[2,32,48,200]{3,2,1,0:T(8,128)(2,1)S(1)}, bf16[2,32,48,200]{3,2,1,0:T(8,128)(2,1)}, u32[]{:S(2)}) copy-start(bf16[2,32,48,200]{3,2,1,0:T(8,128)(2,1)} %param.5) | copy-start | bytes 3686404
  7.3 11.0 %collective-permute-start = (bf16[48,254]{1,0:T(8,128)(2,1)S(1)}, bf16[48,254]{1,0:T(8,128)(2,1)S(1)}, u32[]{:S(2)}, u32[]{:S(2)}) collective-permute-start(bf16[48,254]{1,0:T(8,128)(2,1)S(1)} %slice.52), channel_id=1, source_target_pairs={{1,0},{2,1},{3,2},{4,3},{5,4},{6,5},{7,6},{9,8},{10,9},{11,10},{12... | collective-permute-start | bytes 73160 | tf_op jit(solution)/shard_map/ppermute | solution.py:14
  26.6 0.8 copy-start.3
  26.6 1.1 copy-start.4
  162.6 3.9 %copy-start = (f32[1536,384]{0,1:T(8,128)S(1)}, f32[1536,384]{0,1:T(8,128)}, u32[]{:S(2)}) copy-start(f32[1536,384]{0,1:T(8,128)} %get-tuple-element.8) | copy-start | bytes 7077892
  168.5 2.4 %copy-start.1 = (f32[1536,384]{0,1:T(8,128)S(1)}, f32[1536,384]{0,1:T(8,128)}, u32[]{:S(2)}) copy-start(f32[1536,384]{0,1:T(8,128)} %get-tuple-element.5) | copy-start | bytes 7077892
  172.8 2.0 %copy-start.2 = (f32[512,384]{1,0:T(8,128)S(1)}, f32[512,384]{1,0:T(8,128)}, u32[]{:S(2)}) copy-start(f32[512,384]{1,0:T(8,128)} %get-tuple-element.24) | copy-start | bytes 2359300
Sparse Core Ops, SparseCore 0:
  19.8 64.5 all-gather.1
where the time goes:
time: 186 us; the launch traced here: 185 us
  other arithmetic  69.9 us (38%)
  waiting for transfers between devices  56 us (30%)
  local copies, waits for them, and re-layouts  31.5 us (17%)
  between operations  13.6 us (7%)
  matrix products  13 us (7%)
    all_gather x1, waiting for transfers between devices, per_device(): lax.all_gather(window, 'tmpl', axis=0, tiled=True)  46.4 us
    sub x2, other arithmetic, detect(): prod_a * c_theta - prod_b * s_theta  27.1 us
    add x2, other arithmetic, detect(): prod_a * s_theta + prod_b * c_theta  20.6 us
    gather x4, local copies, waits for them, and re-layouts, detect(): picked = spectra[chans.reshape(-1)].astype(jnp.float32)  18.4 us
    ppermute x1, waiting for transfers between devices, from_behind(): return lax.ppermute(block, axis, route)  9.56 us
    dot_general x2, matrix products, detect(): jnp.dot(waves.reshape(-1, waves.shape[2]), forward[:waves.shape[2]], pref...  5.98 us
    add x2, local copies, waits for them, and re-layouts, detect(): prod_a * s_theta + prod_b * c_theta  5.11 us
    another operation x1, other arithmetic  5 us
  transfers between devices with their start and end apart: 2, of which 2 were waited for; matrix products, arithmetic and copies ran while one was open for 9% of the time, Pallas kernels for 0%

commit v1 on v0

--- a/solution.py
+++ b/solution.py
@@ -1,11 +1,26 @@
+import functools
 import math
 import jax
 import jax.numpy as jnp
 from jax import lax
 from jax.sharding import PartitionSpec as P
+from jax.lax import all_to_all, axis_size
 
 L = 200
 LAGS = 56
+
+
+def cover_racks_for(mat, d_out):
+    prior = jnp.concatenate(
+        all_to_all(
+            jnp.stack([mat for _ in range(axis_size("tmpl"))]), "tmpl", concat_axis=0, split_axis=0
+        ),
+        d_out,
+    )
+    return prior
+
+
+bind_sites_on = functools.partial(cover_racks_for, d_out=0)
 
 
 def from_behind(block, axis, distance):
@@ -59,11 +74,9 @@
     weight = jnp.where((freq == 0) | (freq == freqs - 1), 1.0, 2.0).astype(jnp.float32) / width
     rim = from_behind(records[:, :extra], "tm", -1)
     window = jnp.concatenate([records, rim], axis=1)
-    spectra = jnp.dot(
-        lax.all_gather(window, "tmpl", axis=0, tiled=True),
-        forward,
-        preferred_element_type=jnp.float32,
-    ).astype(jnp.bfloat16)
+    spectra = jnp.dot(bind_sites_on(window), forward, preferred_element_type=jnp.float32).astype(
+        jnp.bfloat16
+    )
     results = []
     for batch in range(templates.shape[0]):
         results.append(

time: 186 us -> 175 us (0.941)
  between operations: 13.6 us -> 0.24 us
  starting transfers between devices: 1.41 us -> 10.2 us
  waiting for transfers between devices: 56 us -> 47.9 us
    all_gather x1 -> x0, waiting for transfers between devices: 46.4 us -> none  [per_device(): lax.all_gather(window, 'tmpl', axis=0, tiled=True)]
    all_to_all x0 -> x1, waiting for transfers between devices: none -> 38.4 us  [cover_racks_for(): all_to_all(jnp.stack([mat for _ in range(axis_size('tmpl'))]), 'tmpl', co...]
    all_to_all x0 -> x1, starting transfers between devices: none -> 8.92 us  [cover_racks_for(): all_to_all(jnp.stack([mat for _ in range(axis_size('tmpl'))]), 'tmpl', co...]
where the time goes in v1:
time: 175 us; the launch traced here: 174 us
  other arithmetic  69.3 us (40%)
  waiting for transfers between devices  47.9 us (27%)
  local copies, waits for them, and re-layouts  33 us (19%)
  matrix products  13 us (7%)
  starting transfers between devices  10.2 us (6%)
    all_to_all x1, waiting for transfers between devices, cover_racks_for(): all_to_all(jnp.stack([mat for _ in range(axis_size('tmpl'))]), 'tmpl', co...  38.4 us
    sub x2, other arithmetic, detect(): prod_a * c_theta - prod_b * s_theta  27.1 us
    add x2, other arithmetic, detect(): prod_a * s_theta + prod_b * c_theta  20.6 us
    gather x4, local copies, waits for them, and re-layouts, detect(): picked = spectra[chans.reshape(-1)].astype(jnp.float32)  18.4 us
    ppermute x1, waiting for transfers between devices, from_behind(): return lax.ppermute(block, axis, route)  9.56 us
    all_to_all x1, starting transfers between devices, cover_racks_for(): all_to_all(jnp.stack([mat for _ in range(axis_size('tmpl'))]), 'tmpl', co...  8.92 us
    dot_general x2, matrix products, detect(): jnp.dot(waves.reshape(-1, waves.shape[2]), forward[:waves.shape[2]], pref...  5.99 us
    add x2, local copies, waits for them, and re-layouts, detect(): prod_a * s_theta + prod_b * c_theta  5.13 us
  transfers between devices with their start and end apart: 2, of which 2 were waited for; matrix products, arithmetic and copies ran while one was open for 9% of the time, Pallas kernels for 0%

profile of v1, /device:TPU:1, one launch (start us, length us, event | category | flops | bytes accessed | tf_op | source)
XLA Modules:
  0.0 173.7 jit_solution(13296419147776490798)
XLA Ops:
  2.0 9.6 %collective-permute-done = bf16[48,254]{1,0:T(8,128)(2,1)S(1)} collective-permute-done((bf16[48,254]{1,0:T(8,128)(2,1)S(1)}, bf16[48,254]{1,0:T(8,128)(2,1)S(1)}, u32[]{:S(2)}, u32[]{:S(2)}) %collective-permute-start) | collective-permute-done | bytes 24416 | tf_op jit(solution)/shard_map/ppermute | solution.py:29
  13.9 8.9 %all-to-all-start = ((bf16[32,48,766]{2,1,0:T(8,128)(2,1)}), bf16[32,48,766]{2,1,0:T(8,128)(2,1)S(1)}, u32[]{:S(2)}, u32[]{:S(2)}) async-start(bf16[32,48,766]{2,1,0:T(8,128)(2,1)} %stack.8), calls=%async_computation | async-start | bytes 4718592 | tf_op jit(solution)/shard_map/all_to_all | solution.py:15
  23.4 5.0 %sine_convert_fusion = (bf16[766,384]{1,0:T(8,128)(2,1)S(1)}, bf16[766,384]{1,0:T(8,128)(2,1)S(1)}) fusion(), kind=kLoop, calls=%fused_computation.41 | loop fusion | flops 3235584 | bytes 1176576 | tf_op jit(solution)/shard_map/convert.1
  29.4 4.2 %fusion.30 = (f32[512,384]{1,0:T(8,128)S(1)}, f32[512,384]{1,0:T(8,128)}) fusion(), kind=kLoop, calls=%fused_computation.54 | loop fusion | flops 1769472 | bytes 1572864 | tf_op jit(solution)/shard_map/sin | solution.py:36
  33.8 3.0 %convolution_bitcast_fusion = f32[1536,768]{0,1:T(8,128)} fusion(bf16[200,768]{1,0:T(8,128)(2,1)S(1)} %pad_maximum_fusion.7, bf16[1536,200]{1,0:T(8,128)(2,1)S(1)} %bitcast.25), kind=kOutput, calls=%fused_computation.2 | convolution fusion | flops 471859200 | bytes 5640192 | tf_op jit(solution)/shard_map/dot_general | solution.py:41
  36.8 3.0 %convolution_bitcast_fusion.1 = f32[1536,768]{0,1:T(8,128)} fusion(bf16[200,768]{1,0:T(8,128)(2,1)S(1)} %pad_maximum_fusion.7, bf16[1536,200]{1,0:T(8,128)(2,1)S(1)} %bitcast.24), kind=kOutput, calls=%fused_computation.3 | convolution fusion | flops 471859200 | bytes 5640192 | tf_op jit(solution)/shard_map/dot_general | solution.py:41
  39.7 38.4 %all-to-all-done = bf16[32,48,766]{2,1,0:T(8,128)(2,1)S(1)} async-done(((bf16[32,48,766]{2,1,0:T(8,128)(2,1)}), bf16[32,48,766]{2,1,0:T(8,128)(2,1)S(1)}, u32[]{:S(2)}, u32[]{:S(2)}) %all-to-all-start) | async-done | bytes 2353184 | tf_op jit(solution)/shard_map/all_to_all | solution.py:15
  79.5 4.0 %convolution_convert_fusion = bf16[1536,768]{1,0:T(8,128)(2,1)S(1)} fusion(bf16[1536,766]{1,0:T(8,128)(2,1)} %bitcast.26, bf16[766,384]{1,0:T(8,128)(2,1)} %copy-done.4, bf16[766,384]{1,0:T(8,128)(2,1)} %copy-done.5), kind=kOutput, calls=%fused_computation.6 | convolution fusion | flops 1810753536 | bytes 5889024 | tf_op jit(solution)/shard_map/dot_general | solution.py:77
  83.5 5.7 %gather_fusion.1 = bf16[1536,768]{1,0:T(8,128)(2,1)} fusion(bf16[1536,768]{1,0:T(8,128)(2,1)S(1)} %convolution_convert_fusion, s32[2048]{0:T(1024)S(1)} %pad_clamp_fusion), kind=kCustom, calls=%fused_computation.1 | custom fusion | bytes 4724736 | tf_op jit(solution)/shard_map/gather | solution.py:54
  89.1 4.3 %copy.10 = bf16[1536,768]{0,1:T(8,128)(2,1)} copy(bf16[1536,768]{1,0:T(8,128)(2,1)} %gather_fusion.1) | data formatting | bytes 4718592 | tf_op jit(solution)/shard_map/gather | solution.py:54
  93.4 2.3 %convert_element_type.31 = f32[1536,768]{0,1:T(8,128)S(1)} convert(bf16[1536,768]{0,1:T(8,128)(2,1)} %copy.10) | non-fusion elementwise | flops 1179648 | bytes 7077888 | tf_op jit(solution)/shard_map/convert_element_type | solution.py:54
  95.7 13.5 %multiply_subtract_fusion = (f32[1536,384]{0,1:T(8,128)}, f32[1536,384]{0,1:T(8,128)S(1)}, f32[1536,384]{0,1:T(8,128)S(1)}) fusion(s32[1536]{0:T(1024)S(1)} %mul.198, f32[1536,768]{0,1:T(8,128)S(1)} %convert_element_type.31, f32[1536,768]{0,1:T(8,128)} %convolution_bitcast_fusion), kind=kLoop, calls=%fused_computation.12 | loop fusion | flops 10616832 | bytes 16521216 | tf_op jit(solution)/shard_map/sub | solution.py:58
  109.3 10.8 %multiply_add_fusion = f32[1536,384]{0,1:T(8,128)} fusion(f32[1536,384]{0,1:T(8,128)S(1)} %get-tuple-element.10, f32[1536,384]{0,1:T(8,128)S(1)} %get-tuple-element.9, s32[1536]{0:T(1024)S(1)} %mul.198), kind=kLoop, calls=%fused_computation.11 | loop fusion | flops 7077888 | bytes 7084032 | tf_op jit(solution)/shard_map/add | solution.py:59
  120.0 3.1 %copy.12 = f32[1536,384]{1,0:T(8,128)} copy(f32[1536,384]{0,1:T(8,128)} %multiply_add_fusion) | data formatting | bytes 4718592 | tf_op jit(solution)/shard_map/add | solution.py:59
  123.2 5.7 %gather_fusion = bf16[1536,768]{1,0:T(8,128)(2,1)} fusion(bf16[1536,768]{1,0:T(8,128)(2,1)S(1)} %convolution_convert_fusion, s32[2048]{0:T(1024)S(1)} %pad_clamp_fusion.1), kind=kCustom, calls=%fused_computation | custom fusion | bytes 4724736 | tf_op jit(solution)/shard_map/gather | solution.py:54
  128.9 2.8 %copy.7 = bf16[1536,768]{0,1:T(8,128)(2,1)S(1)} copy(bf16[1536,768]{1,0:T(8,128)(2,1)} %gather_fusion) | data formatting | bytes 4718592 | tf_op jit(solution)/shard_map/gather | solution.py:54
  132.3 13.5 %multiply_subtract_fusion.2 = (f32[1536,384]{0,1:T(8,128)}, f32[1536,384]{0,1:T(8,128)S(1)}, f32[1536,384]{0,1:T(8,128)S(1)}) fusion(s32[1536]{0:T(1024)S(1)} %mul.177, f32[1536,768]{0,1:T(8,128)S(1)} %convert_element_type.28, f32[1536,768]{0,1:T(8,128)} %convolution_bitcast_fusion.1), kind=kLoop, calls=%fused_computation.21 | loop fusion | flops 10616832 | bytes 16521216 | tf_op jit(solution)/shard_map/sub | solution.py:58
  145.9 9.9 %multiply_add_fusion.2 = f32[1536,384]{0,1:T(8,128)S(1)} fusion(f32[1536,384]{0,1:T(8,128)S(1)} %get-tuple-element.7, f32[1536,384]{0,1:T(8,128)S(1)} %get-tuple-element.6, s32[1536]{0:T(1024)S(1)} %mul.177), kind=kLoop, calls=%fused_computation.20 | loop fusion | flops 7077888 | bytes 7084032 | tf_op jit(solution)/shard_map/add | solution.py:59
  155.7 2.0 %copy.9 = f32[1536,384]{1,0:T(8,128)} copy(f32[1536,384]{0,1:T(8,128)S(1)} %multiply_add_fusion.2) | data formatting | bytes 4718592 | tf_op jit(solution)/shard_map/add | solution.py:59
  157.7 2.0 %reduce_sum.39 = f32[32,384]{1,0:T(8,128)S(1)} reduce(f32[32,48,384]{2,1,0:T(8,128)} %bitcast.20, f32[]{:T(128)} %constant.26.clone.1), dimensions={1}, to_apply=%region_3.4 | reduce | flops 577536 | bytes 2408452 | tf_op jit(solution)/shard_map/reduce_sum | solution.py:59
  161.6 2.0 %copy.11 = f32[1536,384]{1,0:T(8,128)} copy(f32[1536,384]{0,1:T(8,128)S(1)} %copy-done) | data formatting | bytes 4718592 | tf_op jit(solution)/shard_map/sub | solution.py:58
  163.6 2.0 %reduce_sum.38 = f32[32,384]{1,0:T(8,128)S(1)} reduce(f32[32,48,384]{2,1,0:T(8,128)} %bitcast.23, f32[]{:T(128)} %constant.26.clone.1), dimensions={1}, to_apply=%region_2.3 | reduce | flops 577536 | bytes 2408452 | tf_op jit(solution)/shard_map/reduce_sum | solution.py:58
  166.0 2.0 %copy.8 = f32[1536,384]{1,0:T(8,128)} copy(f32[1536,384]{0,1:T(8,128)S(1)} %copy-done.1) | data formatting | bytes 4718592 | tf_op jit(solution)/shard_map/sub | solution.py:58
  168.0 1.9 %reduce_sum.36 = f32[32,384]{1,0:T(8,128)S(1)} reduce(f32[32,48,384]{2,1,0:T(8,128)} %bitcast.22, f32[]{:T(128)} %constant.26.clone.1), dimensions={1}, to_apply=%region_0.1 | reduce | flops 577536 | bytes 2408452 | tf_op jit(solution)/shard_map/reduce_sum | solution.py:58
  (41 shorter events, 13.9 us)
Async XLA Ops:
  0.7 10.8 %collective-permute-start = (bf16[48,254]{1,0:T(8,128)(2,1)S(1)}, bf16[48,254]{1,0:T(8,128)(2,1)S(1)}, u32[]{:S(2)}, u32[]{:S(2)}) collective-permute-start(bf16[48,254]{1,0:T(8,128)(2,1)S(1)} %slice.52), channel_id=1, source_target_pairs={{1,0},{2,1},{3,2},{4,3},{5,4},{6,5},{7,6},{9,8},{10,9},{11,10},{12... | collective-permute-start | bytes 73160 | tf_op jit(solution)/shard_map/ppermute | solution.py:29
  13.9 8.9 %copy-start.7 = (s32[2,32,48]{2,1,0:T(8,128)S(1)}, s32[2,32,48]{2,1,0:T(8,128)}, u32[]{:S(2)}) copy-start(s32[2,32,48]{2,1,0:T(8,128)} %param.6) | copy-start | bytes 36868
  13.9 9.0 %copy-start.8 = (s32[2,32,48]{2,1,0:T(8,128)S(1)}, s32[2,32,48]{2,1,0:T(8,128)}, u32[]{:S(2)}) copy-start(s32[2,32,48]{2,1,0:T(8,128)} %param.7) | copy-start | bytes 36868
  13.9 64.2 %all-to-all-start = ((bf16[32,48,766]{2,1,0:T(8,128)(2,1)}), bf16[32,48,766]{2,1,0:T(8,128)(2,1)S(1)}, u32[]{:S(2)}, u32[]{:S(2)}) async-start(bf16[32,48,766]{2,1,0:T(8,128)(2,1)} %stack.8), calls=%async_computation | async-start | bytes 4718592 | tf_op jit(solution)/shard_map/all_to_all | solution.py:15
  23.2 10.4 %copy-start.6 = (bf16[2,32,48,200]{3,2,1,0:T(8,128)(2,1)S(1)}, bf16[2,32,48,200]{3,2,1,0:T(8,128)(2,1)}, u32[]{:S(2)}) copy-start(bf16[2,32,48,200]{3,2,1,0:T(8,128)(2,1)} %param.5) | copy-start | bytes 3686404
  28.4 0.8 copy-start.4
  28.4 1.0 copy-start.5
  78.1 1.4 copy-start.3
  157.7 3.9 %copy-start = (f32[1536,384]{0,1:T(8,128)S(1)}, f32[1536,384]{0,1:T(8,128)}, u32[]{:S(2)}) copy-start(f32[1536,384]{0,1:T(8,128)} %get-tuple-element.8) | copy-start | bytes 7077892
  163.6 2.4 %copy-start.1 = (f32[1536,384]{0,1:T(8,128)S(1)}, f32[1536,384]{0,1:T(8,128)}, u32[]{:S(2)}) copy-start(f32[1536,384]{0,1:T(8,128)} %get-tuple-element.5) | copy-start | bytes 7077892
  168.0 2.0 %copy-start.2 = (f32[512,384]{1,0:T(8,128)S(1)}, f32[512,384]{1,0:T(8,128)}, u32[]{:S(2)}) copy-start(f32[512,384]{1,0:T(8,128)} %get-tuple-element.24) | copy-start | bytes 2359300
